TPU v7x, 128 devices: a whole 4x4x4 slice. The times are simulated.
128 devices in a mesh: req: 16 (over y, x), seq: 4 (over z), hid: 2 (over core).
Axes of the slice: x: 4, y: 4, z: 4, core: 2. Of those that a mesh axis runs over, the one named last changes fastest.
Arguments:
- tokens: bfloat16 [65536, 2048], P(('req', 'seq')), may hold values from -6 to 6
- attention_gain: bfloat16 [2048], replicated, may hold values from 0.099609375 to 1.8984375
- project_weight: bfloat16 [2048, 2048], P(None, 'hid'), may hold values from -0.125 to 0.125
- conv_weight: bfloat16 [4, 2048], P(None, 'hid'), may hold values from -3 to 3
- decay_down: bfloat16 [2048, 16], replicated, may hold values from -0.125 to 0.125
- decay_up: bfloat16 [16, 512], P(None, 'hid'), may hold values from -1.5 to 1.5
- decay_bias: float32 [512], P('hid'), may hold values from -2 to 10
- output_gate: bfloat16 [2048, 1024], P(None, 'hid'), may hold values from -0.125 to 0.125
- head_gain: bfloat16 [512], replicated, may hold values from 0.099609375 to 1.8984375
- output_weight: bfloat16 [1024, 2048], P('hid'), may hold values from -0.1875 to 0.1875
- mixer_gain: bfloat16 [2048], replicated, may hold values from 0.099609375 to 1.8984375
- gate_weight: bfloat16 [2048, 2816], P('req', 'hid'), may hold values from -0.125 to 0.125
- up_weight: bfloat16 [2048, 2816], P('req', 'hid'), may hold values from -0.125 to 0.125
- down_weight: bfloat16 [2816, 2048], P('hid', 'req'), may hold values from -0.109375 to 0.109375
- prompt_pages: int32 [16, 16], P('req'), may hold values from 0 to 64, as said below
- prompt_start: int32 [16, 16], P('req'), may hold values from 0 to 63, as said below
Outputs:
- hidden_out: bfloat16 [65536, 2048], P(('req', 'seq', 'hid'))
- page_states: bfloat16 [1024, 2, 256, 512], P(('req', 'seq'), 'hid')
- conv_edges: bfloat16 [1024, 3, 2048], P(('req', 'seq'), None, 'hid')
Inputs may be any that keep to these rules, and one draw needn't show every extreme that they name: `prompt_pages`: row r lists the page counts of the prompts of group r; 0 marks an unused slot; in every draw some group holds one prompt of all its 64 pages. `prompt_start`: the slots of a row that are used cover pages in increasing order without intersection and end by page 64; pages between prompts belong to none; an unused slot starts at page 64 - 1, and every draw has one.
All inputs are finite; a program needn't handle non-finite values.
Results may differ from a plain program's by a relative error of at most 0.014.
Values may be sent and summed in bfloat16 or wider, within the bound.
A program may use at most 192 MiB of HBM per device.

v0:
```python
import jax
import jax.numpy as jnp
from jax import lax
from jax.sharding import PartitionSpec as P

HK = 256
HV = 512
KCONV = 4
PAGE = 64
CONVW = 1024
EPSILON = 1e-06
TOP_PRECISION = lax.Precision.HIGHEST


def shifted(value, axis, steps):
    count = lax.axis_size(axis)
    first, last = (max(0, -steps), min(count, count - steps))
    return lax.ppermute(value, axis, [(source, source + steps) for source in range(first, last)])


def prefix_2(array, axis, join, neutral):
    place = lax.axis_index(axis)
    gathered = jax.tree.map(
        lambda a, kind: lax.all_gather(a.astype(kind), axis), array, (jnp.bfloat16, jnp.bfloat16)
    )
    state = jax.tree.map(lambda a, e: jnp.zeros_like(a) + jnp.asarray(e, a.dtype), array, neutral)

    def one(lap, state):
        return join(
            state,
            jax.tree.map(
                lambda a, own: lax.dynamic_index_in_dim(a, lap, 0, False).astype(own.dtype),
                gathered,
                array,
            ),
        )

    return lax.fori_loop(0, place, one, state)


def rms_scaled(values, scale_gain):
    values = values.astype(jnp.float32)
    return (
        values
        * lax.rsqrt(jnp.mean(values * values, axis=-1, keepdims=True) + EPSILON)
        * scale_gain.astype(jnp.float32)
    )


def page_segments(page_counts, starts, total_pages):
    position = jnp.arange(total_pages, dtype=jnp.int32)
    inside = (position[None, :] >= starts[:, None]) & (
        position[None, :] < starts[:, None] + page_counts[:, None]
    )
    labels = jnp.arange(1, page_counts.shape[0] + 1, dtype=jnp.int32)
    segment = jnp.sum(jnp.where(inside, labels[:, None], 0), axis=0) - 1
    earlier = jnp.concatenate([jnp.full((1,), -1, jnp.int32), segment[:-1]])
    return ((segment == earlier) & (segment >= 0)).astype(jnp.float32)


def short_conv(by_page, before, carried, conv_taps):
    kept_rows = before.astype(jnp.float32) * carried[:, None, None]
    widened = jnp.concatenate([kept_rows, by_page.astype(jnp.float32)], axis=1)
    tap_count = conv_taps.shape[0]
    length = by_page.shape[1]
    result = jnp.zeros(by_page.shape, jnp.float32)
    for offset in range(tap_count):
        result = (
            result
            + conv_taps[offset].astype(jnp.float32)
            * widened[:, tap_count - 1 - offset : tap_count - 1 - offset + length]
        )
    return result


def split_features(mixed_rows, key_width):
    query_rows = jax.nn.silu(mixed_rows[..., :key_width])
    key_rows = jax.nn.silu(mixed_rows[..., key_width : 2 * key_width]) * key_width ** (-0.5)
    value_matrix = mixed_rows[..., 2 * key_width :]
    return (
        query_rows.transpose(0, 2, 1, 3),
        key_rows.transpose(0, 2, 1, 3),
        value_matrix.transpose(0, 2, 1, 3),
    )


def page_block(query_rows, key_rows, value_matrix, decay_sum, carried):
    length = query_rows.shape[2]
    page_count = query_rows.shape[0]
    raised_rows = query_rows * jnp.exp(decay_sum)
    lowered = key_rows * jnp.exp(-decay_sum)
    scores = jnp.einsum("phik,phjk->phij", raised_rows, lowered, precision=TOP_PRECISION)
    rows_index = jnp.arange(length)
    causal = rows_index[:, None] >= rows_index[None, :]
    scores = jnp.where(causal[None, None], scores, 0.0)
    layer_output = jnp.einsum("phij,phjv->phiv", scores, value_matrix, precision=TOP_PRECISION)
    closing_sum = decay_sum[:, :, -1, :]
    weighted_rows = key_rows * jnp.exp(closing_sum[:, :, None, :] - decay_sum)
    page_terms = jnp.einsum("phte,phtb->pheb", weighted_rows, value_matrix, precision=TOP_PRECISION)
    through = jnp.cumsum(closing_sum, axis=0)
    resets = jnp.cumsum(1.0 - carried)
    pages = jnp.arange(page_count)
    valid = (pages[:, None] >= pages[None, :]) & (resets[:, None] == resets[None, :])
    spread = through[:, None] - through[None, :]
    spread = jnp.where(valid[:, :, None, None], spread, 0.0)
    weights = jnp.where(valid[:, :, None, None], jnp.exp(spread), 0.0)
    memories = jnp.einsum("pqhe,qheb->pheb", weights, page_terms, precision=TOP_PRECISION)
    previous = jnp.concatenate([jnp.zeros_like(memories[:1]), memories[:-1]], axis=0)
    previous = previous * carried[:, None, None, None]
    layer_output = layer_output + jnp.einsum(
        "phik,phkv->phiv", raised_rows, previous, precision=TOP_PRECISION
    )
    return (memories[-1], layer_output, memories)


def on_device(
    tokens,
    attention_gain,
    project_weight,
    conv_weight,
    decay_down,
    decay_up,
    decay_bias,
    output_gate,
    head_gain,
    output_weight,
    mixer_gain,
    gate_weight,
    up_weight,
    down_weight,
    prompt_pages,
    prompt_start,
):
    token_count = tokens.shape[0]
    page_count = token_count // PAGE
    local_heads = project_weight.shape[1] // CONVW
    rim_rows = KCONV - 1
    seq_index = lax.axis_index("seq")
    group_pages = page_count * lax.axis_size("seq")
    page_flags = page_segments(prompt_pages[0], prompt_start[0], group_pages)
    carried = lax.dynamic_slice_in_dim(page_flags, seq_index * page_count, page_count)
    normed = rms_scaled(tokens, attention_gain).astype(jnp.bfloat16)
    projected = jnp.dot(normed, project_weight, preferred_element_type=jnp.float32).astype(
        jnp.bfloat16
    )
    by_page = projected.reshape(page_count, PAGE, local_heads * CONVW)
    incoming = shifted(by_page[-1, PAGE - rim_rows :], "seq", 1)
    before = jnp.concatenate([incoming[None], by_page[:-1, PAGE - rim_rows :]], axis=0)
    mixed_rows = short_conv(by_page, before, carried, conv_weight).reshape(
        page_count, PAGE, local_heads, CONVW
    )
    query_rows, key_rows, value_matrix = split_features(mixed_rows, HK)
    lowrank = jnp.dot(normed, decay_down, preferred_element_type=jnp.float32).astype(jnp.bfloat16)
    decay_log = (
        jax.nn.log_sigmoid(
            jnp.dot(lowrank, decay_up, preferred_element_type=jnp.float32) + decay_bias
        )
        / 16.0
    )
    decay_log = decay_log.reshape(page_count, PAGE, local_heads, HK).transpose(0, 2, 1, 3)
    decay_sum = jnp.cumsum(decay_log, axis=2)
    local_memory, outputs, memories = page_block(
        query_rows, key_rows, value_matrix, decay_sum, carried
    )
    totals = decay_sum[:, :, -1, :]
    through = jnp.cumsum(totals, axis=0)
    alive_mask = jnp.cumprod(carried)
    block_decay = alive_mask[-1] * jnp.exp(through[-1])

    def compose(earlier, latter):
        return (earlier[0] * latter[0], latter[0][..., None] * earlier[1] + latter[1])

    prefix = prefix_2(
        (block_decay, local_memory),
        "seq",
        compose,
        (jnp.ones_like(block_decay), jnp.zeros_like(local_memory)),
    )
    incoming_state = prefix[1]
    before_sum = through - totals
    extent_factor = alive_mask[:, None, None, None] * jnp.exp(decay_sum + before_sum[:, :, None, :])
    outputs = outputs + jnp.einsum(
        "dlof,lfg->dlog", query_rows * extent_factor, incoming_state, precision=TOP_PRECISION
    )
    memories = (
        memories + (alive_mask[:, None, None] * jnp.exp(through))[..., None] * incoming_state[None]
    )
    attended = outputs.transpose(0, 2, 1, 3).reshape(token_count, local_heads, HV)
    normed_heads = rms_scaled(attended, head_gain)
    opening = jax.nn.silu(jnp.dot(normed, output_gate, preferred_element_type=jnp.float32)).reshape(
        token_count, local_heads, HV
    )
    gated_rows = (
        (normed_heads * opening).astype(jnp.bfloat16).reshape(token_count, local_heads * HV)
    )
    partial_value = jnp.dot(gated_rows, output_weight, preferred_element_type=jnp.float32)
    half_rows = token_count // lax.axis_size("hid")
    row_start = lax.axis_index("hid") * half_rows
    mixed_sum = lax.psum(partial_value.astype(jnp.bfloat16), "hid").astype(jnp.float32)
    residual = (tokens.astype(jnp.float32) + mixed_sum).astype(jnp.bfloat16)
    feed_in = rms_scaled(residual, mixer_gain).astype(jnp.bfloat16)
    own_residual = lax.dynamic_slice_in_dim(residual, row_start, half_rows, 0)

    def widen(weight_rows):
        return jnp.dot(feed_in, weight_rows, preferred_element_type=jnp.float32)

    gate_part = widen(lax.all_gather(gate_weight, "req", axis=0, tiled=True))
    up_part = widen(lax.all_gather(up_weight, "req", axis=0, tiled=True))
    hidden = (jax.nn.silu(gate_part) * up_part).astype(jnp.bfloat16)
    partials = jnp.dot(
        hidden,
        lax.all_gather(down_weight, "req", axis=1, tiled=True),
        preferred_element_type=jnp.float32,
    )
    feed_sum = lax.psum_scatter(
        partials.astype(jnp.bfloat16), "hid", scatter_dimension=0, tiled=True
    ).astype(jnp.float32)
    result = (own_residual.astype(jnp.float32) + feed_sum).astype(jnp.bfloat16)
    return (result, memories.astype(jnp.bfloat16), by_page[:, PAGE - rim_rows :])


def solution(mesh):
    return jax.shard_map(
        on_device,
        mesh=mesh,
        in_specs=(
            P(("req", "seq"), None),
            P(),
            P(None, "hid"),
            P(None, "hid"),
            P(),
            P(None, "hid"),
            P("hid"),
            P(None, "hid"),
            P(),
            P("hid", None),
            P(),
            P("req", "hid"),
            P("req", "hid"),
            P("hid", "req"),
            P("req", None),
            P("req", None),
        ),
        out_specs=(
            P(("req", "seq", "hid"), None),
            P(("req", "seq"), "hid", None, None),
            P(("req", "seq"), None, "hid"),
        ),
        check_vma=False,
    )
```

profile of v0, /device:TPU:1, one launch (start us, length us, event | category | flops | bytes accessed | tf_op | source)
XLA Modules:
  0.0 364.4 jit_solution(5683534701682440027)
XLA Ops:
  11.7 7.3 %convolution_convert_fusion.2 = bf16[1024,1024]{1,0:T(8,128)(2,1)S(1)} fusion(bf16[2048,1024]{1,0:T(8,128)(2,1)} %param.20, bf16[1024,2048]{1,0:T(8,128)(2,1)S(1)} %copy-done.6, f32[2048]{0:T(1024)S(1)} %convert_element_type.149, f32[1024]{0:T(1024)S(1)} %add_rsqrt_fusion.2), kind=kOutput, calls=%fused_computation.53 | convolution fusion | flops 4304404480 | bytes 10498048 | tf_op jit(solution)/shard_map/dot_general | solution.py:143
  20.3 4.4 %collective-permute-start = (bf16[3,1024]{1,0:T(4,128)(2,1)S(1)}, bf16[3,1024]{1,0:T(4,128)(2,1)S(1)}, u32[]{:S(2)}, u32[]{:S(2)}) collective-permute-start(bf16[3,1024]{1,0:T(4,128)(2,1)S(1)} %slice_bitcast_fusion.5), channel_id=1, source_target_pairs={{0,2},{2,4},{4,6},{1,3},{3,5},{5,7},{8,10},{10,12},{12,14},{9,11},... | collective-permute-start | bytes 18440 | tf_op jit(solution)/shard_map/ppermute | solution.py:18
  24.9 5.2 %fusion.37 = f32[1024,256]{1,0:T(8,128)} fusion(bf16[16,256]{1,0:T(8,128)(2,1)S(1)} %copy-done.15, bf16[2048,16]{0,1:T(8,128)(2,1)S(1)} %copy-done.14, f32[256]{0:T(256)S(1)} %copy-done.16, bf16[1024,2048]{1,0:T(8,128)(2,1)} %param.18, f32[2048]{0:T(1024)S(1)} %convert_element_type.149, f32[1024]{0:T(1024)S(1)} %add_rsqrt_fusion.2), kind=kOutput, calls=%fused_computation.60 | convolution fusion | flops 86523904 | bytes 5329920 | tf_op jit(solution)/shard_map/dot_general | solution.py:156
  34.8 4.1 %convert_element_type.152 = f32[16,64,1024]{2,1,0:T(8,128)} convert(bf16[16,64,1024]{2,1,0:T(8,128)(2,1)} %bitcast.138) | non-fusion elementwise | flops 1048576 | bytes 6291456 | tf_op jit(solution)/shard_map/convert_element_type | solution.py:63
  39.1 6.9 %all_gather.17 = bf16[4,1,256]{2,1,0:T(2,128)(2,1)S(1)} all-gather(bf16[1,1,256]{2,1,0:T(2,128)(2,1)S(1)} %fusion.71), channel_id=1, replica_groups=mesh['req'=16,'seq'=4,'hid'=2] {'seq'}, dimensions={0}, use_global_device_ids=true | all-gather | bytes 2560 | tf_op jit(solution)/shard_map/all_gather | solution.py:24
  46.1 7.6 %fusion.15 = f32[16,64,1,1024]{3,1,0,2:T(8,128)S(1)} fusion(f32[16,64,1024]{2,1,0:T(8,128)} %convert_element_type.152, f32[16,3,1024]{2,1,0:T(4,128)S(1)} %convert_multiply_fusion.4, f32[1024]{0:T(1024)S(1)} %bitcast.145, f32[1024]{0:T(1024)S(1)} %bitcast.146, f32[1024]{0:T(1024)S(1)} %bitcast.144, f32[1024]{0:T(1024)S(1)} %bitcast.143), kind=kLoop, calls=%fused_computation.29 | loop fusion | flops 10485760 | bytes 8601600 | tf_op jit(solution)/shard_map/reshape | solution.py:149
  53.7 7.4 %fusion.30 = f32[16,256,512]{2,1,0:T(8,128)S(1)} fusion(f32[16,64,1,1024]{3,1,0,2:T(8,128)S(1)} %fusion.15, f32[16,1,64,256]{3,0,1,2:T(8,128)S(1)} %fusion.48, f32[16,256]{1,0:T(8,128)S(1)} %get-tuple-element.85), kind=kOutput, calls=%fused_computation.51 | convolution fusion | flops 1612447744 | bytes 12599296 | tf_op jit(solution)/shard_map/phte,phtb->pheb/dot_general | solution.py:99
  61.1 13.6 %fusion.20 = f32[16,1,256,512]{3,0,2,1:T(8,128)S(1)} fusion(f32[16,256,512]{2,1,0:T(8,128)S(1)} %fusion.30, f32[16,256]{0,1:T(8,128)S(1)} %bitcast.140, pred[16,16]{1,0:T(8,128)(4,1)S(1)} %fusion.69), kind=kOutput, calls=%fused_computation.38 | convolution fusion | flops 402849792 | bytes 16793856 | tf_op jit(solution)/shard_map/pqhe,qheb->pheb/dot_general | solution.py:107
  79.5 4.2 %convolution_select_fusion = f32[16,64,64]{2,1,0:T(8,128)S(1)} fusion(f32[16,1,64,256]{3,0,1,2:T(8,128)S(1)} %fusion.48, pred[64,64]{1,0:T(8,128)(4,1)S(1)} %iota_compare_fusion, f32[16,64,1,1024]{3,1,0,2:T(8,128)} %copy-done.3), kind=kOutput, calls=%fused_computation.56 | convolution fusion | flops 204537856 | bytes 4464640 | tf_op jit(solution)/shard_map/phik,phjk->phij/dot_general | solution.py:92
  86.9 5.3 %multiply_bitcast_fusion = f32[16,256,512]{2,0,1:T(8,128)S(1)} fusion(f32[15,1,256,512]{3,0,2,1:T(8,128)} %bitcast.134, f32[16]{0:T(128)S(1)} %get-tuple-element.83), kind=kLoop, calls=%fused_computation.19 | loop fusion | flops 2097152 | bytes 16252992 | tf_op jit(solution)/shard_map/reshape.33
  92.3 13.1 %fusion.7 = f32[16,64,512]{2,1,0:T(8,128)} fusion(f32[16,256,512]{2,0,1:T(8,128)S(1)} %multiply_bitcast_fusion, f32[16,1,64,256]{3,0,1,2:T(8,128)S(1)} %fusion.48, f32[16,64,1,1024]{3,1,0,2:T(8,128)} %copy-done.3), kind=kOutput, calls=%fused_computation.14 | convolution fusion | flops 1611923456 | bytes 12582912 | tf_op jit(solution)/shard_map/phik,phkv->phiv/dot_general | solution.py:110
  105.5 6.8 %multiply_reduce_fusion = (f32[16,64]{1,0:T(8,128)S(1)}, f32[16,1,64,512]{3,2,0,1:T(8,128)}) fusion(f32[16,1,64,256]{3,0,1,2:T(8,128)} %copy-done.5, f32[16,256]{1,0:T(8,128)S(1)} %get-tuple-element.84, f32[16]{0:T(128)S(1)} %reduce.3, f32[16,64,1,1024]{3,1,0,2:T(8,128)} %copy-done.3, f32[1,256,512]{2,1,0:T(8,128)S(1)} %get-tuple-element.47, ...), kind=kOutput, calls=%fused_computation.46 | convolution fusion | flops 1614543872 | bytes 8933440 | tf_op jit(solution)/shard_map/dlof,lfg->dlog/dot_general | solution.py:182
  112.4 6.2 %fusion.25 = bf16[1024,512]{1,0:T(8,128)(2,1)S(1)} fusion(f32[16,1,64,512]{3,2,0,1:T(8,128)} %get-tuple-element.91, f32[512]{0:T(512)S(1)} %convert_element_type.163, f32[1024]{0:T(1024)S(1)} %rsqrt.29, bf16[2048,512]{1,0:T(8,128)(2,1)} %param.25, bf16[1024,2048]{1,0:T(8,128)(2,1)} %param.18, f32[2048]{0:T(1024)S(1)} %convert_element_type.149, ...), kind=kOutput, calls=%fused_computation.45 | convolution fusion | flops 2160066560 | bytes 9455616 | tf_op jit(solution)/shard_map/dot_general | solution.py:190
  118.5 4.4 %convolution_convert_fusion.1 = bf16[1024,2048]{1,0:T(8,128)(2,1)} fusion(bf16[1024,512]{1,0:T(8,128)(2,1)S(1)} %fusion.25, bf16[512,2048]{1,0:T(8,128)(2,1)S(1)} %copy-done), kind=kOutput, calls=%fused_computation.37 | convolution fusion | flops 2149580800 | bytes 7340032 | tf_op jit(solution)/shard_map/dot_general | solution.py:196
  125.0 37.7 %all-reduce.3.cloned.1.call-done = bf16[1024,2048]{1,0:T(8,128)(2,1)} async-done(((bf16[1024,2048]{1,0:T(8,128)(2,1)}), bf16[1024,2048]{1,0:T(8,128)(2,1)}) %all-reduce.3.cloned.1.call-update) | async-done | bytes 4194320 | tf_op jit(solution)/shard_map/psum | solution.py:199
  162.7 7.7 %fusion = (f32[1024]{0:T(1024)S(1)}, bf16[1024,2048]{1,0:T(8,128)(2,1)}) fusion(bf16[1024,2048]{1,0:T(8,128)(2,1)} %all-reduce.3.cloned.1.call-done, bf16[1024,2048]{1,0:T(8,128)(2,1)} %param.18), kind=kLoop, calls=%fused_computation.7 | loop fusion | flops 14679040 | bytes 12587008 | tf_op jit(solution)/shard_map/reduce_sum | solution.py:45
  170.4 19.1 %all-gather.7.cloned.1.call-done = bf16[2048,1408]{1,0:T(8,128)(2,1)} async-done(((bf16[128,1408]{1,0:T(8,128)(2,1)}), bf16[2048,1408]{1,0:T(8,128)(2,1)}) %all-gather.7.cloned.1.call-update) | async-done | bytes 5767184 | tf_op jit(solution)/shard_map/all_gather | solution.py:207
  189.4 12.0 %fusion.34 = f32[1024,1408]{1,0:T(8,128)} fusion(bf16[2048,1408]{1,0:T(8,128)(2,1)} %all-gather.7.cloned.1.call-done, bf16[1024,2048]{1,0:T(8,128)(2,1)} %get-tuple-element.81, f32[2048]{0:T(1024)S(1)} %convert_element_type.170, f32[1024]{0:T(1024)S(1)} %add_rsqrt_fusion.1), kind=kOutput, calls=%fused_computation.57 | convolution fusion | flops 5913968640 | bytes 15740928 | tf_op jit(solution)/shard_map/dot_general | solution.py:205
  201.4 53.5 %all-gather.11.cloned.1.call-done = bf16[1408,2048]{1,0:T(8,128)(2,1)} async-done(((bf16[1408,128]{1,0:T(8,128)(2,1)}), bf16[1408,2048]{1,0:T(8,128)(2,1)}) %all-gather.11.cloned.1.call-update) | async-done | bytes 5767184 | tf_op jit(solution)/shard_map/all_gather | solution.py:212
  254.9 61.3 %all-gather.9.cloned.1.call-done = bf16[2048,1408]{1,0:T(8,128)(2,1)} async-done(((bf16[128,1408]{1,0:T(8,128)(2,1)}), bf16[2048,1408]{1,0:T(8,128)(2,1)}) %all-gather.9.cloned.1.call-update) | async-done | bytes 5767184 | tf_op jit(solution)/shard_map/all_gather | solution.py:208
  316.1 20.9 %convolution_convert_fusion = bf16[1024,2048]{1,0:T(8,128)(2,1)} fusion(bf16[1408,2048]{1,0:T(8,128)(2,1)} %all-gather.11.cloned.1.call-done, f32[1024,1408]{1,0:T(8,128)} %fusion.34, bf16[2048,1408]{1,0:T(8,128)(2,1)} %all-gather.9.cloned.1.call-done, bf16[1024,2048]{1,0:T(8,128)(2,1)} %get-tuple-element.81, f32[2048]{0:T(1024)S(1)} %convert_element_type.170, ...), kind=kOutput, calls=%fused_computation.36 | convolution fusion | flops 11830296576 | bytes 25702400 | tf_op jit(solution)/shard_map/dot_general | solution.py:210
  342.9 4.4 %copy.71 = bf16[16,1,256,512]{3,2,1,0:T(8,128)(2,1)} copy(bf16[16,1,256,512]{3,0,2,1:T(8,128)(2,1)S(1)} %add_convert_fusion) | data formatting | bytes 8388608
  347.3 4.8 %reduce-scatter.2.cloned.1.call-done = bf16[512,2048]{1,0:T(8,128)(2,1)} async-done(((bf16[1024,2048]{1,0:T(8,128)(2,1)}), bf16[512,2048]{1,0:T(8,128)(2,1)}) %reduce-scatter.2.cloned.1.call-update) | async-done | bytes 2097168 | tf_op jit(solution)/shard_map/reduce_scatter | solution.py:215
  352.1 4.4 %add_convert_fusion.1 = bf16[512,2048]{1,0:T(8,128)(2,1)} fusion(bf16[512,2048]{1,0:T(8,128)(2,1)} %reduce-scatter.2.cloned.1.call-done, bf16[1024,2048]{1,0:T(8,128)(2,1)} %get-tuple-element.81, s32[]{:T(128)S(6)} %select_n.46), kind=kLoop, calls=%fused_computation.35 | loop fusion | flops 4194304 | bytes 6291460 | tf_op jit(solution)/shard_map/convert_element_type | solution.py:218
  (90 shorter events, 26.0 us)
Async XLA Ops:
  8.0 110.5 %copy-start = (bf16[512,2048]{1,0:T(8,128)(2,1)S(1)}, bf16[512,2048]{1,0:T(8,128)(2,1)}, u32[]{:S(2)}) copy-start(bf16[512,2048]{1,0:T(8,128)(2,1)} %param.27) | copy-start | bytes 6291460
  8.0 3.3 copy-start.9
  8.0 97.4 %all-gather.5.cloned.1.call-start = ((), (), s32[]{:S(2)}) async-start(), calls=%async_computation.1 | async-start | bytes 1310720 | tf_op jit(solution)/shard_map/all_gather | solution.py:24
  8.1 3.6 copy-start.6
  11.6 13.0 %copy-start.11 = (s32[1,16]{1,0:T(1,128)S(1)}, s32[1,16]{1,0:T(1,128)}, u32[]{:S(2)}) copy-start(s32[1,16]{1,0:T(1,128)} %param.33) | copy-start | bytes 196
  11.6 13.0 %copy-start.13 = (s32[1,16]{1,0:T(1,128)S(1)}, s32[1,16]{1,0:T(1,128)}, u32[]{:S(2)}) copy-start(s32[1,16]{1,0:T(1,128)} %param.32) | copy-start | bytes 196
  11.6 13.2 %copy-start.8 = (bf16[4,1024]{1,0:T(4,128)(2,1)S(1)}, bf16[4,1024]{1,0:T(4,128)(2,1)}, u32[]{:S(2)}) copy-start(bf16[4,1024]{1,0:T(4,128)(2,1)} %param.21) | copy-start | bytes 24580
  11.6 13.2 %copy-start.14 = (bf16[2048,16]{0,1:T(8,128)(2,1)S(1)}, bf16[2048,16]{0,1:T(8,128)(2,1)}, u32[]{:S(2)}) copy-start(bf16[2048,16]{0,1:T(8,128)(2,1)} %param.22) | copy-start | bytes 196612
  11.6 13.2 %copy-start.15 = (bf16[16,256]{1,0:T(8,128)(2,1)S(1)}, bf16[16,256]{1,0:T(8,128)(2,1)}, u32[]{:S(2)}) copy-start(bf16[16,256]{1,0:T(8,128)(2,1)} %param.23) | copy-start | bytes 24580
  11.7 13.2 %copy-start.16 = (f32[256]{0:T(256)S(1)}, f32[256]{0:T(256)}, u32[]{:S(2)}) copy-start(f32[256]{0:T(256)} %param.24) | copy-start | bytes 3076
  18.9 1.3 copy-start.7
  20.3 25.7 %collective-permute-start = (bf16[3,1024]{1,0:T(4,128)(2,1)S(1)}, bf16[3,1024]{1,0:T(4,128)(2,1)S(1)}, u32[]{:S(2)}, u32[]{:S(2)}) collective-permute-start(bf16[3,1024]{1,0:T(4,128)(2,1)S(1)} %slice_bitcast_fusion.5), channel_id=1, source_target_pairs={{0,2},{2,4},{4,6},{1,3},{3,5},{5,7},{8,10},{10,12},{12,14},{9,11},... | collective-permute-start | bytes 18440 | tf_op jit(solution)/shard_map/ppermute | solution.py:18
  30.0 9.0 %copy-start.12 = (bf16[512]{0:T(512)(128)(2,1)S(1)}, bf16[512]{0:T(512)(128)(2,1)}, u32[]{:S(2)}) copy-start(bf16[512]{0:T(512)(128)(2,1)} %param.26) | copy-start | bytes 3076
  31.9 60.4 %copy-start.5 = (f32[16,1,64,256]{3,0,1,2:T(8,128)}, f32[16,1,64,256]{3,0,1,2:T(8,128)S(1)}, u32[]{:S(2)}) copy-start(f32[16,1,64,256]{3,0,1,2:T(8,128)S(1)} %fusion.48) | copy-start | bytes 3145732
  53.7 7.4 %copy-start.3 = (f32[16,64,1,1024]{3,1,0,2:T(8,128)}, f32[16,64,1,1024]{3,1,0,2:T(8,128)S(1)}, u32[]{:S(2)}) copy-start(f32[16,64,1,1024]{3,1,0,2:T(8,128)S(1)} %fusion.15) | copy-start | bytes 12582916
  74.7 3.2 copy-start.2
  79.3 83.3 %all-reduce.3.cloned.1.call-start = ((), (), s32[]{:S(2)}) async-start(), calls=%async_computation.2 | async-start | bytes 8388608 | tf_op jit(solution)/shard_map/psum | solution.py:199
  79.5 4.2 %copy-start.4 = (f32[16,64,1,1024]{3,1,0,2:T(8,128)S(1)}, f32[16,64,1,1024]{3,1,0,2:T(8,128)}, u32[]{:S(2)}) copy-start(f32[16,64,1,1024]{3,1,0,2:T(8,128)} %copy-done.3) | copy-start | bytes 12582916
  122.9 2.1 copy-start.10
  122.9 66.5 %all-gather.7.cloned.1.call-start = ((), (), s32[]{:S(2)}) async-start(), calls=%async_computation.3 | async-start | bytes 6127616 | tf_op jit(solution)/shard_map/all_gather | solution.py:207
  123.5 131.4 %all-gather.11.cloned.1.call-start = ((), (), s32[]{:S(2)}) async-start(), calls=%async_computation.5 | async-start | bytes 6127616 | tf_op jit(solution)/shard_map/all_gather | solution.py:212
  124.1 192.1 %all-gather.9.cloned.1.call-start = ((), (), s32[]{:S(2)}) async-start(), calls=%async_computation.4 | async-start | bytes 6127616 | tf_op jit(solution)/shard_map/all_gather | solution.py:208
  124.7 227.5 %reduce-scatter.2.cloned.1.call-start = ((), (), s32[]{:S(2)}) async-start(), calls=%async_computation.6 | async-start | bytes 6291456 | tf_op jit(solution)/shard_map/reduce_scatter | solution.py:215
  342.9 13.7 %copy-start.1 = (bf16[512,2048]{1,0:T(8,128)(2,1)S(1)}, bf16[512,2048]{1,0:T(8,128)(2,1)}, u32[]{:S(2)}) copy-start(bf16[512,2048]{1,0:T(8,128)(2,1)} %param.27) | copy-start | bytes 6291460
Sparse Core Ops, SparseCore 0:
  79.4 24.9 all-gather.4
  123.0 39.5 all-reduce.2
  337.2 14.9 reduce-scatter.1
Sparse Core Ops, SparseCore 1:
  125.7 63.6 all-gather.6
  191.6 63.2 all-gather.10
  257.1 59.0 all-gather.8
where the time goes:
time: 371 us; the launch traced here: 364 us
  waiting for transfers between devices  178 us (48%)
  matrix products  104 us (28%)
  other arithmetic  39.8 us (11%)
  between operations  16.3 us (4%)
  local copies, waits for them, and re-layouts  14.4 us (4%)
  blocking collectives  6.9 us (2%)
  starting transfers between devices  5.04 us (1%)
    all_gather x1, waiting for transfers between devices, on_device(): up_part = widen(lax.all_gather(up_weight, 'req', axis=0, tiled=True))  61.3 us
    all_gather x1, waiting for transfers between devices, on_device(): lax.all_gather(down_weight, 'req', axis=1, tiled=True)  53.5 us
    psum x1, waiting for transfers between devices, on_device(): lax.psum(partial_value.astype(jnp.bfloat16), 'hid').astype(jnp.float32)  37.7 us
    dot_general x1, matrix products, on_device(): jnp.dot(hidden, lax.all_gather(down_weight, 'req', axis=1, tiled=True), p...  20.9 us
    all_gather x1, waiting for transfers between devices, on_device(): gate_part = widen(lax.all_gather(gate_weight, 'req', axis=0, tiled=True))  19.1 us
    dot_general x1, matrix products, page_block(): jnp.einsum('pqhe,qheb->pheb', weights, page_terms, precision=TOP_PRECISION)  13.6 us
    dot_general x1, matrix products, page_block(): jnp.einsum('phik,phkv->phiv', raised_rows, previous, precision=TOP_PRECIS...  13.1 us
    dot_general x1, matrix products, widen(): return jnp.dot(feed_in, weight_rows, preferred_element_type=jnp.float32)  12 us
  transfers between devices with their start and end apart: 7, of which 5 were waited for; matrix products, arithmetic and copies ran while one was open for 19% of the time, Pallas kernels for 0%

commit v1 on v0

--- a/solution.py
+++ b/solution.py
@@ -10,6 +10,14 @@
 CONVW = 1024
 EPSILON = 1e-06
 TOP_PRECISION = lax.Precision.HIGHEST
+
+
+def gather_by_exchange(shard, axis, dim):
+    size = lax.axis_size(axis)
+    repeats = [size if d == dim else 1 for d in range(shard.ndim)]
+    return lax.all_to_all(
+        jnp.tile(shard, repeats), axis, split_axis=dim, concat_axis=dim, tiled=True
+    )
 
 
 def shifted(value, axis, steps):
@@ -204,7 +212,7 @@
     def widen(weight_rows):
         return jnp.dot(feed_in, weight_rows, preferred_element_type=jnp.float32)
 
-    gate_part = widen(lax.all_gather(gate_weight, "req", axis=0, tiled=True))
+    gate_part = widen(gather_by_exchange(gate_weight, "req", 0))
     up_part = widen(lax.all_gather(up_weight, "req", axis=0, tiled=True))
     hidden = (jax.nn.silu(gate_part) * up_part).astype(jnp.bfloat16)
     partials = jnp.dot(

time: 371 us -> 368 us (level)
  waiting for transfers between devices: 178 us -> 165 us
  starting transfers between devices: 5.04 us -> 11.9 us
    all_to_all x0 -> x1, waiting for transfers between devices: none -> 48.3 us  [gather_by_exchange(): lax.all_to_all(jnp.tile(shard, repeats), axis, split_axis=dim, concat_axi...]
    all_gather x1, waiting for transfers between devices: 61.3 us -> 15.6 us  [on_device(): up_part = widen(lax.all_gather(up_weight, 'req', axis=0, tiled=True))]
    all_gather x1 -> x0, waiting for transfers between devices: 19.1 us -> none  [on_device(): gate_part = widen(lax.all_gather(gate_weight, 'req', axis=0, tiled=True))]
    all_gather x1, waiting for transfers between devices: 53.5 us -> 66.6 us  [on_device(): lax.all_gather(down_weight, 'req', axis=1, tiled=True)]
    psum x1, waiting for transfers between devices: 37.7 us -> 28.3 us  [on_device(): lax.psum(partial_value.astype(jnp.bfloat16), 'hid').astype(jnp.float32)]
    all_to_all x0 -> x1, starting transfers between devices: none -> 6.94 us  [gather_by_exchange(): lax.all_to_all(jnp.tile(shard, repeats), axis, split_axis=dim, concat_axi...]
    unnamed x37 -> x39, local copies, waits for them, and re-layouts: 10.1 us -> 10.2 us
  transfers between devices with their start and end apart: 7 -> 7, of which waited for: 5 -> 5; matrix products, arithmetic and copies ran while one was open for 19% -> 20% of each run, Pallas kernels for 0% -> 0%
where the time goes in v1:
time: 368 us; the launch traced here: 361 us
  waiting for transfers between devices  165 us (45%)
  matrix products  104 us (28%)
  other arithmetic  39.8 us (11%)
  local copies, waits for them, and re-layouts  17.6 us (5%)
  between operations  15.8 us (4%)
  starting transfers between devices  11.9 us (3%)
  blocking collectives  6.9 us (2%)
    all_gather x1, waiting for transfers between devices, on_device(): lax.all_gather(down_weight, 'req', axis=1, tiled=True)  66.6 us
    all_to_all x1, waiting for transfers between devices, gather_by_exchange(): lax.all_to_all(jnp.tile(shard, repeats), axis, split_axis=dim, concat_axi...  48.3 us
    psum x1, waiting for transfers between devices, on_device(): lax.psum(partial_value.astype(jnp.bfloat16), 'hid').astype(jnp.float32)  28.3 us
    dot_general x1, matrix products, on_device(): jnp.dot(hidden, lax.all_gather(down_weight, 'req', axis=1, tiled=True), p...  20.9 us
    all_gather x1, waiting for transfers between devices, on_device(): up_part = widen(lax.all_gather(up_weight, 'req', axis=0, tiled=True))  15.6 us
    dot_general x1, matrix products, page_block(): jnp.einsum('phik,phkv->phiv', raised_rows, previous, precision=TOP_PRECIS...  13.4 us
    dot_general x1, matrix products, page_block(): jnp.einsum('pqhe,qheb->pheb', weights, page_terms, precision=TOP_PRECISION)  13.4 us
    dot_general x1, matrix products, widen(): return jnp.dot(feed_in, weight_rows, preferred_element_type=jnp.float32)  12 us
  transfers between devices with their start and end apart: 7, of which 5 were waited for; matrix products, arithmetic and copies ran while one was open for 20% of the time, Pallas kernels for 0%

profile of v1, /device:TPU:1, one launch (start us, length us, event | category | flops | bytes accessed | tf_op | source)
XLA Modules:
  0.0 361.3 jit_solution(7442710649853216804)
XLA Ops:
  11.7 7.3 %convolution_convert_fusion.2 = bf16[1024,1024]{1,0:T(8,128)(2,1)S(1)} fusion(bf16[2048,1024]{1,0:T(8,128)(2,1)} %param.20, bf16[1024,2048]{1,0:T(8,128)(2,1)S(1)} %copy-done.6, f32[2048]{0:T(1024)S(1)} %convert_element_type.149, f32[1024]{0:T(1024)S(1)} %add_rsqrt_fusion.2), kind=kOutput, calls=%fused_computation.53 | convolution fusion | flops 4304404480 | bytes 10498048 | tf_op jit(solution)/shard_map/dot_general | solution.py:151
  20.3 4.4 %collective-permute-start = (bf16[3,1024]{1,0:T(4,128)(2,1)S(1)}, bf16[3,1024]{1,0:T(4,128)(2,1)S(1)}, u32[]{:S(2)}, u32[]{:S(2)}) collective-permute-start(bf16[3,1024]{1,0:T(4,128)(2,1)S(1)} %slice_bitcast_fusion.5), channel_id=1, source_target_pairs={{0,2},{2,4},{4,6},{1,3},{3,5},{5,7},{8,10},{10,12},{12,14},{9,11},... | collective-permute-start | bytes 18440 | tf_op jit(solution)/shard_map/ppermute | solution.py:26
  24.9 5.2 %fusion.37 = f32[1024,256]{1,0:T(8,128)} fusion(bf16[16,256]{1,0:T(8,128)(2,1)S(1)} %copy-done.16, bf16[2048,16]{0,1:T(8,128)(2,1)S(1)} %copy-done.15, f32[256]{0:T(256)S(1)} %copy-done.17, bf16[1024,2048]{1,0:T(8,128)(2,1)} %param.18, f32[2048]{0:T(1024)S(1)} %convert_element_type.149, f32[1024]{0:T(1024)S(1)} %add_rsqrt_fusion.2), kind=kOutput, calls=%fused_computation.60 | convolution fusion | flops 86523904 | bytes 5329920 | tf_op jit(solution)/shard_map/dot_general | solution.py:164
  39.1 6.9 %all_gather.14 = bf16[4,1,256]{2,1,0:T(2,128)(2,1)S(1)} all-gather(bf16[1,1,256]{2,1,0:T(2,128)(2,1)S(1)} %fusion.71), channel_id=1, replica_groups=mesh['req'=16,'seq'=4,'hid'=2] {'seq'}, dimensions={0}, use_global_device_ids=true | all-gather | bytes 2560 | tf_op jit(solution)/shard_map/all_gather | solution.py:32
  46.1 7.8 %fusion.15 = f32[16,64,1,1024]{3,1,0,2:T(8,128)S(1)} fusion(f32[16,64,1024]{2,1,0:T(8,128)} %convert_element_type.152, f32[16,3,1024]{2,1,0:T(4,128)S(1)} %convert_multiply_fusion.4, f32[1024]{0:T(1024)S(1)} %bitcast.146, f32[1024]{0:T(1024)S(1)} %bitcast.147, f32[1024]{0:T(1024)S(1)} %bitcast.145, f32[1024]{0:T(1024)S(1)} %bitcast.144), kind=kLoop, calls=%fused_computation.29 | loop fusion | flops 10485760 | bytes 8601600 | tf_op jit(solution)/shard_map/reshape | solution.py:157
  53.9 7.4 %fusion.30 = f32[16,256,512]{2,1,0:T(8,128)S(1)} fusion(f32[16,64,1,1024]{3,1,0,2:T(8,128)S(1)} %fusion.15, f32[16,1,64,256]{3,0,1,2:T(8,128)S(1)} %fusion.48, f32[16,256]{1,0:T(8,128)S(1)} %get-tuple-element.85), kind=kOutput, calls=%fused_computation.51 | convolution fusion | flops 1612447744 | bytes 12599296 | tf_op jit(solution)/shard_map/phte,phtb->pheb/dot_general | solution.py:107
  61.3 13.4 %fusion.20 = f32[16,1,256,512]{3,0,2,1:T(8,128)S(1)} fusion(f32[16,256,512]{2,1,0:T(8,128)S(1)} %fusion.30, f32[16,256]{0,1:T(8,128)S(1)} %bitcast.141, pred[16,16]{1,0:T(8,128)(4,1)S(1)} %fusion.69), kind=kOutput, calls=%fused_computation.38 | convolution fusion | flops 402849792 | bytes 16793856 | tf_op jit(solution)/shard_map/pqhe,qheb->pheb/dot_general | solution.py:115
  79.6 4.2 %convolution_select_fusion = f32[16,64,64]{2,1,0:T(8,128)S(1)} fusion(f32[16,1,64,256]{3,0,1,2:T(8,128)S(1)} %fusion.48, pred[64,64]{1,0:T(8,128)(4,1)S(1)} %iota_compare_fusion, f32[16,64,1,1024]{3,1,0,2:T(8,128)} %copy-done.3), kind=kOutput, calls=%fused_computation.56 | convolution fusion | flops 204537856 | bytes 4464640 | tf_op jit(solution)/shard_map/phik,phjk->phij/dot_general | solution.py:100
  86.9 5.4 %multiply_bitcast_fusion = f32[16,256,512]{2,0,1:T(8,128)S(1)} fusion(f32[15,1,256,512]{3,0,2,1:T(8,128)} %bitcast.135, f32[16]{0:T(128)S(1)} %get-tuple-element.83), kind=kLoop, calls=%fused_computation.19 | loop fusion | flops 2097152 | bytes 16252992 | tf_op jit(solution)/shard_map/reshape.33
  92.3 13.4 %fusion.7 = f32[16,64,512]{2,1,0:T(8,128)} fusion(f32[16,256,512]{2,0,1:T(8,128)S(1)} %multiply_bitcast_fusion, f32[16,1,64,256]{3,0,1,2:T(8,128)S(1)} %fusion.48, f32[16,64,1,1024]{3,1,0,2:T(8,128)} %copy-done.3), kind=kOutput, calls=%fused_computation.14 | convolution fusion | flops 1611923456 | bytes 12582912 | tf_op jit(solution)/shard_map/phik,phkv->phiv/dot_general | solution.py:118
  105.7 6.8 %multiply_reduce_fusion = (f32[16,64]{1,0:T(8,128)S(1)}, f32[16,1,64,512]{3,2,0,1:T(8,128)}) fusion(f32[16,1,64,256]{3,0,1,2:T(8,128)} %copy-done.5, f32[16,256]{1,0:T(8,128)S(1)} %get-tuple-element.84, f32[16]{0:T(128)S(1)} %reduce.3, f32[16,64,1,1024]{3,1,0,2:T(8,128)} %copy-done.3, f32[1,256,512]{2,1,0:T(8,128)S(1)} %get-tuple-element.47, ...), kind=kOutput, calls=%fused_computation.46 | convolution fusion | flops 1614543872 | bytes 8933440 | tf_op jit(solution)/shard_map/dlof,lfg->dlog/dot_general | solution.py:190
  112.6 6.2 %fusion.25 = bf16[1024,512]{1,0:T(8,128)(2,1)S(1)} fusion(f32[16,1,64,512]{3,2,0,1:T(8,128)} %get-tuple-element.91, f32[512]{0:T(512)S(1)} %convert_element_type.163, f32[1024]{0:T(1024)S(1)} %rsqrt.29, bf16[2048,512]{1,0:T(8,128)(2,1)} %param.25, bf16[1024,2048]{1,0:T(8,128)(2,1)} %param.18, f32[2048]{0:T(1024)S(1)} %convert_element_type.149, ...), kind=kOutput, calls=%fused_computation.45 | convolution fusion | flops 2160066560 | bytes 9455616 | tf_op jit(solution)/shard_map/dot_general | solution.py:198
  118.8 4.4 %convolution_convert_fusion.1 = bf16[1024,2048]{1,0:T(8,128)(2,1)} fusion(bf16[1024,512]{1,0:T(8,128)(2,1)S(1)} %fusion.25, bf16[512,2048]{1,0:T(8,128)(2,1)S(1)} %copy-done), kind=kOutput, calls=%fused_computation.37 | convolution fusion | flops 2149580800 | bytes 7340032 | tf_op jit(solution)/shard_map/dot_general | solution.py:204
  127.5 6.9 %all-to-all-start = ((bf16[16,128,1408]{2,1,0:T(8,128)(2,1)}), bf16[16,128,1408]{2,1,0:T(8,128)(2,1)}, u32[]{:S(2)}, u32[]{:S(2)}) async-start(bf16[16,128,1408]{2,1,0:T(8,128)(2,1)} %tile.2), calls=%async_computation | async-start | bytes 11534336 | tf_op jit(solution)/shard_map/all_to_all | solution.py:18
  134.7 28.3 %all-reduce.3.cloned.1.call-done = bf16[1024,2048]{1,0:T(8,128)(2,1)} async-done(((bf16[1024,2048]{1,0:T(8,128)(2,1)}), bf16[1024,2048]{1,0:T(8,128)(2,1)}) %all-reduce.3.cloned.1.call-update) | async-done | bytes 4194320 | tf_op jit(solution)/shard_map/psum | solution.py:207
  163.0 7.5 %fusion = (f32[1024]{0:T(1024)S(1)}, bf16[1024,2048]{1,0:T(8,128)(2,1)}) fusion(bf16[1024,2048]{1,0:T(8,128)(2,1)} %all-reduce.3.cloned.1.call-done, bf16[1024,2048]{1,0:T(8,128)(2,1)} %param.18), kind=kLoop, calls=%fused_computation.7 | loop fusion | flops 14679040 | bytes 12587008 | tf_op jit(solution)/shard_map/reduce_sum | solution.py:53
  170.4 48.3 %all-to-all-done = bf16[16,128,1408]{2,1,0:T(8,128)(2,1)} async-done(((bf16[16,128,1408]{2,1,0:T(8,128)(2,1)}), bf16[16,128,1408]{2,1,0:T(8,128)(2,1)}, u32[]{:S(2)}, u32[]{:S(2)}) %all-to-all-start) | async-done | bytes 5767200 | tf_op jit(solution)/shard_map/all_to_all | solution.py:18
  218.7 12.0 %fusion.34 = f32[1024,1408]{1,0:T(8,128)} fusion(bf16[2048,1408]{1,0:T(8,128)(2,1)} %bitcast.35, bf16[1024,2048]{1,0:T(8,128)(2,1)} %get-tuple-element.81, f32[2048]{0:T(1024)S(1)} %convert_element_type.170, f32[1024]{0:T(1024)S(1)} %add_rsqrt_fusion.1), kind=kOutput, calls=%fused_computation.57 | convolution fusion | flops 5913968640 | bytes 15740928 | tf_op jit(solution)/shard_map/dot_general | solution.py:213
  230.7 15.6 %all-gather.6.cloned.1.call-done = bf16[2048,1408]{1,0:T(8,128)(2,1)} async-done(((bf16[128,1408]{1,0:T(8,128)(2,1)}), bf16[2048,1408]{1,0:T(8,128)(2,1)}) %all-gather.6.cloned.1.call-update) | async-done | bytes 5767184 | tf_op jit(solution)/shard_map/all_gather | solution.py:216
  246.3 66.6 %all-gather.8.cloned.1.call-done = bf16[1408,2048]{1,0:T(8,128)(2,1)} async-done(((bf16[1408,128]{1,0:T(8,128)(2,1)}), bf16[1408,2048]{1,0:T(8,128)(2,1)}) %all-gather.8.cloned.1.call-update) | async-done | bytes 5767184 | tf_op jit(solution)/shard_map/all_gather | solution.py:220
  312.8 20.9 %convolution_convert_fusion = bf16[1024,2048]{1,0:T(8,128)(2,1)} fusion(bf16[1408,2048]{1,0:T(8,128)(2,1)} %all-gather.8.cloned.1.call-done, f32[1024,1408]{1,0:T(8,128)} %fusion.34, bf16[2048,1408]{1,0:T(8,128)(2,1)} %all-gather.6.cloned.1.call-done, bf16[1024,2048]{1,0:T(8,128)(2,1)} %get-tuple-element.81, f32[2048]{0:T(1024)S(1)} %convert_element_type.170, ...), kind=kOutput, calls=%fused_computation.36 | convolution fusion | flops 11830296576 | bytes 25702400 | tf_op jit(solution)/shard_map/dot_general | solution.py:218
  339.6 4.5 %copy.71 = bf16[16,1,256,512]{3,2,1,0:T(8,128)(2,1)} copy(bf16[16,1,256,512]{3,0,2,1:T(8,128)(2,1)S(1)} %add_convert_fusion) | data formatting | bytes 8388608
  344.1 5.4 %reduce-scatter.2.cloned.1.call-done = bf16[512,2048]{1,0:T(8,128)(2,1)} async-done(((bf16[1024,2048]{1,0:T(8,128)(2,1)}), bf16[512,2048]{1,0:T(8,128)(2,1)}) %reduce-scatter.2.cloned.1.call-update) | async-done | bytes 2097168 | tf_op jit(solution)/shard_map/reduce_scatter | solution.py:223
  349.5 4.4 %add_convert_fusion.1 = bf16[512,2048]{1,0:T(8,128)(2,1)} fusion(bf16[512,2048]{1,0:T(8,128)(2,1)} %reduce-scatter.2.cloned.1.call-done, bf16[1024,2048]{1,0:T(8,128)(2,1)} %get-tuple-element.81, s32[]{:T(128)S(6)} %select_n.46), kind=kLoop, calls=%fused_computation.35 | loop fusion | flops 4194304 | bytes 6291460 | tf_op jit(solution)/shard_map/convert_element_type | solution.py:226
  (92 shorter events, 32.7 us)
Async XLA Ops:
  8.0 110.8 %copy-start = (bf16[512,2048]{1,0:T(8,128)(2,1)S(1)}, bf16[512,2048]{1,0:T(8,128)(2,1)}, u32[]{:S(2)}) copy-start(bf16[512,2048]{1,0:T(8,128)(2,1)} %param.27) | copy-start | bytes 6291460
  8.0 3.3 copy-start.10
  8.0 97.6 %all-gather.4.cloned.1.call-start = ((), (), s32[]{:S(2)}) async-start(), calls=%async_computation.2 | async-start | bytes 1310720 | tf_op jit(solution)/shard_map/all_gather | solution.py:32
  8.1 3.6 copy-start.6
  11.6 13.0 %copy-start.12 = (s32[1,16]{1,0:T(1,128)S(1)}, s32[1,16]{1,0:T(1,128)}, u32[]{:S(2)}) copy-start(s32[1,16]{1,0:T(1,128)} %param.33) | copy-start | bytes 196
  11.6 13.0 %copy-start.14 = (s32[1,16]{1,0:T(1,128)S(1)}, s32[1,16]{1,0:T(1,128)}, u32[]{:S(2)}) copy-start(s32[1,16]{1,0:T(1,128)} %param.32) | copy-start | bytes 196
  11.6 13.2 %copy-start.9 = (bf16[4,1024]{1,0:T(4,128)(2,1)S(1)}, bf16[4,1024]{1,0:T(4,128)(2,1)}, u32[]{:S(2)}) copy-start(bf16[4,1024]{1,0:T(4,128)(2,1)} %param.21) | copy-start | bytes 24580
  11.6 13.2 %copy-start.15 = (bf16[2048,16]{0,1:T(8,128)(2,1)S(1)}, bf16[2048,16]{0,1:T(8,128)(2,1)}, u32[]{:S(2)}) copy-start(bf16[2048,16]{0,1:T(8,128)(2,1)} %param.22) | copy-start | bytes 196612
  11.6 13.2 %copy-start.16 = (bf16[16,256]{1,0:T(8,128)(2,1)S(1)}, bf16[16,256]{1,0:T(8,128)(2,1)}, u32[]{:S(2)}) copy-start(bf16[16,256]{1,0:T(8,128)(2,1)} %param.23) | copy-start | bytes 24580
  11.7 13.2 %copy-start.17 = (f32[256]{0:T(256)S(1)}, f32[256]{0:T(256)}, u32[]{:S(2)}) copy-start(f32[256]{0:T(256)} %param.24) | copy-start | bytes 3076
  18.9 1.3 copy-start.7
  20.3 25.7 %collective-permute-start = (bf16[3,1024]{1,0:T(4,128)(2,1)S(1)}, bf16[3,1024]{1,0:T(4,128)(2,1)S(1)}, u32[]{:S(2)}, u32[]{:S(2)}) collective-permute-start(bf16[3,1024]{1,0:T(4,128)(2,1)S(1)} %slice_bitcast_fusion.5), channel_id=1, source_target_pairs={{0,2},{2,4},{4,6},{1,3},{3,5},{5,7},{8,10},{10,12},{12,14},{9,11},... | collective-permute-start | bytes 18440 | tf_op jit(solution)/shard_map/ppermute | solution.py:26
  30.0 9.0 %copy-start.13 = (bf16[512]{0:T(512)(128)(2,1)S(1)}, bf16[512]{0:T(512)(128)(2,1)}, u32[]{:S(2)}) copy-start(bf16[512]{0:T(512)(128)(2,1)} %param.26) | copy-start | bytes 3076
  31.9 60.4 %copy-start.5 = (f32[16,1,64,256]{3,0,1,2:T(8,128)}, f32[16,1,64,256]{3,0,1,2:T(8,128)S(1)}, u32[]{:S(2)}) copy-start(f32[16,1,64,256]{3,0,1,2:T(8,128)S(1)} %fusion.48) | copy-start | bytes 3145732
  53.9 7.4 %copy-start.3 = (f32[16,64,1,1024]{3,1,0,2:T(8,128)}, f32[16,64,1,1024]{3,1,0,2:T(8,128)S(1)}, u32[]{:S(2)}) copy-start(f32[16,64,1,1024]{3,1,0,2:T(8,128)S(1)} %fusion.15) | copy-start | bytes 12582916
  74.7 3.2 copy-start.2
  79.3 83.7 %all-reduce.3.cloned.1.call-start = ((), (), s32[]{:S(2)}) async-start(), calls=%async_computation.3 | async-start | bytes 8388608 | tf_op jit(solution)/shard_map/psum | solution.py:207
  79.5 4.2 %copy-start.4 = (f32[16,64,1,1024]{3,1,0,2:T(8,128)S(1)}, f32[16,64,1,1024]{3,1,0,2:T(8,128)}, u32[]{:S(2)}) copy-start(f32[16,64,1,1024]{3,1,0,2:T(8,128)} %copy-done.3) | copy-start | bytes 12582916
  123.2 123.1 %all-gather.6.cloned.1.call-start = ((), (), s32[]{:S(2)}) async-start(), calls=%async_computation.4 | async-start | bytes 6127616 | tf_op jit(solution)/shard_map/all_gather | solution.py:216
  123.8 189.1 %all-gather.8.cloned.1.call-start = ((), (), s32[]{:S(2)}) async-start(), calls=%async_computation.5 | async-start | bytes 6127616 | tf_op jit(solution)/shard_map/all_gather | solution.py:220
  127.5 7.2 %copy-start.11 = (bf16[2048]{0:T(1024)(128)(2,1)S(1)}, bf16[2048]{0:T(1024)(128)(2,1)}, u32[]{:S(2)}) copy-start(bf16[2048]{0:T(1024)(128)(2,1)} %param.28) | copy-start | bytes 12292
  127.5 91.2 %all-to-all-start = ((bf16[16,128,1408]{2,1,0:T(8,128)(2,1)}), bf16[16,128,1408]{2,1,0:T(8,128)(2,1)}, u32[]{:S(2)}, u32[]{:S(2)}) async-start(bf16[16,128,1408]{2,1,0:T(8,128)(2,1)} %tile.2), calls=%async_computation | async-start | bytes 11534336 | tf_op jit(solution)/shard_map/all_to_all | solution.py:18
  134.5 215.1 %reduce-scatter.2.cloned.1.call-start = ((), (), s32[]{:S(2)}) async-start(), calls=%async_computation.6 | async-start | bytes 6291456 | tf_op jit(solution)/shard_map/reduce_scatter | solution.py:223
  339.6 14.3 %copy-start.1 = (bf16[512,2048]{1,0:T(8,128)(2,1)S(1)}, bf16[512,2048]{1,0:T(8,128)(2,1)}, u32[]{:S(2)}) copy-start(bf16[512,2048]{1,0:T(8,128)(2,1)} %param.27) | copy-start | bytes 6291460
  (1 other events, 1.2 us)
Sparse Core Ops, SparseCore 0:
  79.4 24.9 all-gather.3
  123.3 39.6 all-reduce.2
  333.9 15.6 reduce-scatter.1
Sparse Core Ops, SparseCore 1:
  126.0 120.2 all-gather.5
  248.5 64.3 all-gather.7
